TPU v7x, 32 devices: a whole 2x2x4 slice. The times are simulated.
32 devices in a mesh: sector: 4 (over y, x), term: 8 (over z, core).
Axes of the slice: x: 2, y: 2, z: 4, core: 2. Of those that a mesh axis runs over, the one named last changes fastest.
Arguments:
- wavefunction: float32 [4, 256, 256], P('sector'), may hold values from -6 to 6
- left_env: float32 [384, 256, 256], P(('sector', 'term')), may hold values from -0.0390625 to 0.0390625
- right_env: float32 [384, 256, 256], P(('sector', 'term')), may hold values from -0.375 to 0.375
- in_sector: int32 [384], P(('sector', 'term')), may hold values from 0 to 3
- out_sector: int32 [384], P(('sector', 'term')), may hold values from 0 to 3
- precond: float32 [4, 256, 256], P('sector'), may hold values from 2 to 4
- shifts: float32 [2], replicated, may hold values from 0.2 to 1
Outputs:
- corrected: float32 [4, 256, 256], P('sector')
- residual_norms: float32 [2], replicated
All inputs are finite; a program needn't handle non-finite values.
Results may differ from a plain program's by a relative error of at most 0.0001.
Values sent between devices are 32-bit elements; how exact they have to be, the bound alone decides.
A program may use at most 64 MiB of HBM per device.

v0:
```python
import jax
import jax.numpy as jnp
from jax import lax
from jax.sharding import PartitionSpec as P

ITERS = 2


def apply_tasks(full, left_env, right_env, in_sector, out_sector):

    def one_task(total, item):
        left, right, source, target = item
        block = lax.dynamic_index_in_dim(full, source, 0, keepdims=False)
        middle = jnp.dot(
            left, block, precision=lax.Precision.HIGHEST, preferred_element_type=jnp.float32
        )
        result = jnp.dot(
            middle, right, precision=lax.Precision.HIGHEST, preferred_element_type=jnp.float32
        )
        current = lax.dynamic_index_in_dim(total, target, 0, keepdims=False)
        total = lax.dynamic_update_index_in_dim(total, current + result, target, 0)
        return (total, None)

    start = jnp.zeros(full.shape, jnp.float32)
    total, _ = lax.scan(one_task, start, (left_env, right_env, in_sector, out_sector))
    return total


def correction(sigma, psi, precond, shift):
    residual = sigma - shift * psi
    updated = psi - residual / (precond - shift)
    return (updated, jnp.sum(residual * residual), jnp.sum(updated * updated))


def per_device(wavefunction, left_env, right_env, in_sector, out_sector, precond, shifts):
    full = lax.all_gather(wavefunction, "sector", axis=0, tiled=True)
    norms = []
    psi = wavefunction
    count = lax.axis_size("sector") * psi.size
    for step in range(ITERS):
        partial_value = apply_tasks(full, left_env, right_env, in_sector, out_sector)
        owned = lax.psum_scatter(partial_value, "sector", scatter_dimension=0, tiled=True)
        sigma = lax.psum(owned, "term")
        updated, res_sq, upd_sq = correction(sigma, psi, precond, shifts[step])
        res_total, upd_total = lax.psum((res_sq, upd_sq), "sector")
        norms.append(jnp.sqrt(res_total))
        psi = updated / jnp.sqrt(upd_total / count + 1e-06)
        if step + 1 < ITERS:
            full = lax.all_gather(psi, "sector", axis=0, tiled=True)
    return (psi, jnp.stack(norms))


def solution(mesh):
    placed = (
        P("sector", None, None),
        P(("sector", "term"), None, None),
        P(("sector", "term"), None, None),
        P(("sector", "term")),
        P(("sector", "term")),
        P("sector", None, None),
        P(),
    )
    return jax.shard_map(
        per_device,
        mesh=mesh,
        in_specs=placed,
        out_specs=(P("sector", None, None), P()),
        check_vma=False,
    )
```

profile of v0, /device:TPU:0, one launch (start us, length us, event | category | flops | bytes accessed | tf_op | source)
XLA Modules:
  0.0 478.9 jit_solution(9953802204697645868)
XLA Ops:
  7.9 31.1 %all-gather.3.cloned.1.call-done = f32[4,256,256]{2,1,0:T(8,128)} async-done(((f32[1,256,256]{2,1,0:T(8,128)}), f32[4,256,256]{2,1,0:T(8,128)}) %all-gather.3.cloned.1.call-update) | async-done | bytes 1048592 | tf_op jit(solution)/shard_map/all_gather | solution.py:36
  39.2 110.3 %while.20 = (s32[]{:T(128)}, f32[4,256,256]{2,1,0:T(8,128)S(1)}, s32[12]{0:T(128)}, f32[12,256,256]{2,1,0:T(8,128)}, s32[12]{0:T(128)}, /*index=5*/f32[4,256,256...) while((s32[]{:T(128)}, f32[4,256,256]{2,1,0:T(8,128)S(1)}, s32[12]{0:T(128)}, ...), condition=%wide.region_1.2_spmd, body=%wide.region_0.1_spmd.sunk | while | flops 402718720 | bytes 2360525 | solution.py:25
  39.2 1.3 dynamic_slice.82
  42.4 1.4 fusion.41
  43.9 1.2 dynamic_slice.81
  47.1 1.3 fusion.42
  51.6 1.4 fusion.41
  53.1 1.2 dynamic_slice.81
  56.3 1.3 fusion.42
  60.8 1.4 fusion.41
  65.5 1.3 fusion.42
  70.0 1.4 fusion.41
  71.4 1.2 dynamic_slice.81
  74.7 1.3 fusion.42
  79.2 1.4 fusion.41
  83.8 1.3 fusion.42
  88.4 1.4 fusion.41
  93.0 1.3 fusion.42
  97.6 1.4 fusion.41
  102.2 1.3 fusion.42
  106.8 1.4 fusion.41
  111.4 1.3 fusion.42
  116.0 1.4 fusion.41
  120.6 1.3 fusion.42
  125.2 1.4 fusion.41
  129.8 1.3 fusion.42
  134.4 1.4 fusion.41
  139.0 1.3 fusion.42
  143.5 1.4 fusion.41
  148.2 1.3 fusion.42
  150.6 28.0 %reduce-scatter.7.cloned.1.call-done = f32[1,256,256]{2,1,0:T(8,128)} async-done(((f32[4,256,256]{2,1,0:T(8,128)}), f32[1,256,256]{2,1,0:T(8,128)}) %reduce-scatter.7.cloned.1.call-update) | async-done | bytes 262160
  179.3 57.1 %all-reduce.6.cloned.1.call-done = f32[1,256,256]{2,1,0:T(8,128)} async-done(((f32[1,256,256]{2,1,0:T(8,128)}), f32[1,256,256]{2,1,0:T(8,128)}) %all-reduce.6.cloned.1.call-update) | async-done | bytes 262160 | tf_op jit(solution)/shard_map/psum | solution.py:43
  236.4 2.4 multiply_reduce_fusion.3
  238.8 10.4 %psum.43 = f32[]{:T(128)} all-reduce(f32[]{:T(128)} %get-tuple-element.111), channel_id=1, replica_groups=mesh['sector'=4,'term'=8] {'sector'}, use_global_device_ids=true, to_apply=%region_5.6 | all-reduce | flops 1 | bytes 8 | tf_op jit(solution)/shard_map/psum | solution.py:45
  250.7 23.8 %all-gather.5.cloned.1.call-done = f32[4,256,256]{2,1,0:T(8,128)} async-done(((f32[1,256,256]{2,1,0:T(8,128)}), f32[4,256,256]{2,1,0:T(8,128)}) %all-gather.5.cloned.1.call-update) | async-done | bytes 1048592 | tf_op jit(solution)/shard_map/all_gather | solution.py:49
  274.7 94.6 %while.21 = (s32[]{:T(128)}, f32[4,256,256]{2,1,0:T(8,128)S(1)}, s32[12]{0:T(128)S(1)}, f32[12,256,256]{2,1,0:T(8,128)}, s32[12]{0:T(128)S(1)}, /*index=5*/f32[4...) while((s32[]{:T(128)}, f32[4,256,256]{2,1,0:T(8,128)S(1)}, ...), condition=%wide.region_7.8_spmd, body=%wide.region_6.7_spmd.sunk | while | flops 402718720 | bytes 2360525 | solution.py:25
  277.2 1.4 fusion.47
  281.2 1.3 fusion.48
  285.1 1.4 fusion.47
  289.1 1.3 fusion.48
  293.0 1.4 fusion.47
  296.9 1.3 fusion.48
  300.8 1.4 fusion.47
  304.8 1.3 fusion.48
  308.7 1.4 fusion.47
  312.7 1.3 fusion.48
  316.6 1.4 fusion.47
  320.6 1.3 fusion.48
  324.5 1.4 fusion.47
  328.5 1.3 fusion.48
  332.4 1.4 fusion.47
  336.4 1.3 fusion.48
  340.2 1.4 fusion.47
  344.2 1.3 fusion.48
  348.1 1.4 fusion.47
  352.1 1.3 fusion.48
  356.0 1.4 fusion.47
  360.0 1.3 fusion.48
  363.9 1.4 fusion.47
  367.9 1.3 fusion.48
  370.3 28.0 %reduce-scatter.9.cloned.1.call-done = f32[1,256,256]{2,1,0:T(8,128)} async-done(((f32[4,256,256]{2,1,0:T(8,128)}), f32[1,256,256]{2,1,0:T(8,128)}) %reduce-scatter.9.cloned.1.call-update) | async-done | bytes 262160
  398.4 57.6 %all-reduce.8.cloned.1.call-done = f32[1,256,256]{2,1,0:T(8,128)} async-done(((f32[1,256,256]{2,1,0:T(8,128)}), f32[1,256,256]{2,1,0:T(8,128)}) %all-reduce.8.cloned.1.call-update) | async-done | bytes 262160 | tf_op jit(solution)/shard_map/psum | solution.py:43
  455.9 2.2 multiply_reduce_fusion.2
  458.2 10.5 %all-reduce.2 = (f32[]{:T(128)}, f32[]{:T(128)}, f32[]{:T(128)}) all-reduce(f32[]{:T(128)} %get-tuple-element.109, f32[]{:T(128)} %get-tuple-element.114, f32[]{:T(128)} %get-tuple-element.113), channel_id=1, replica_groups=mesh['sector'=4,'term'=8] {'sector'}, use_global_device_ids=true, to_apply=%region_11.12 | all-reduce | flops 3 | bytes 24 | tf_op jit(solution)/shard_map/psum | solution.py:45
  (100 shorter events, 45.3 us)
Async XLA Ops:
  7.2 31.9 %all-gather.3.cloned.1.call-start = ((), (), s32[]{:S(2)}) async-start(), calls=%async_computation.2 | async-start | bytes 1310720 | tf_op jit(solution)/shard_map/all_gather | solution.py:36
  7.9 170.7 %reduce-scatter.7.cloned.1.call-start = ((), (), s32[]{:S(2)}) async-start(), calls=%async_computation.6 | async-start | bytes 1310720
  39.2 139.6 %copy-start.4 = (f32[2]{0:T(128)S(1)}, f32[2]{0:T(128)}, u32[]{:S(2)}) copy-start(f32[2]{0:T(128)} %param.17) | copy-start | bytes 28
  39.2 197.2 %copy-start.2 = (f32[1,256,256]{2,1,0:T(8,128)S(1)}, f32[1,256,256]{2,1,0:T(8,128)}, u32[]{:S(2)}) copy-start(f32[1,256,256]{2,1,0:T(8,128)} %param.11) | copy-start | bytes 786436
  39.2 197.2 %copy-start.3 = (f32[1,256,256]{2,1,0:T(8,128)S(1)}, f32[1,256,256]{2,1,0:T(8,128)}, u32[]{:S(2)}) copy-start(f32[1,256,256]{2,1,0:T(8,128)} %param.16) | copy-start | bytes 786436
  149.5 1.0 copy-start.1
  149.6 125.1 %copy-start.5 = (s32[12]{0:T(128)S(1)}, s32[12]{0:T(128)}, u32[]{:S(2)}) copy-start(s32[12]{0:T(128)} %get-tuple-element.289) | copy-start | bytes 148
  149.6 125.1 %copy-start.6 = (s32[12]{0:T(128)S(1)}, s32[12]{0:T(128)}, u32[]{:S(2)}) copy-start(s32[12]{0:T(128)} %get-tuple-element.290) | copy-start | bytes 148
  150.5 85.9 %all-reduce.6.cloned.1.call-start = ((), (), s32[]{:S(2)}) async-start(), calls=%async_computation.3 | async-start | bytes 524288 | tf_op jit(solution)/shard_map/psum | solution.py:43
  178.7 95.9 %all-gather.5.cloned.1.call-start = ((), (), s32[]{:S(2)}) async-start(), calls=%async_computation.4 | async-start | bytes 1310720 | tf_op jit(solution)/shard_map/all_gather | solution.py:49
  250.7 147.7 %reduce-scatter.9.cloned.1.call-start = ((), (), s32[]{:S(2)}) async-start(), calls=%async_computation.7 | async-start | bytes 1310720
  369.2 1.0 copy-start
  370.2 85.7 %all-reduce.8.cloned.1.call-start = ((), (), s32[]{:S(2)}) async-start(), calls=%async_computation.5 | async-start | bytes 524288 | tf_op jit(solution)/shard_map/psum | solution.py:43
Sparse Core Ops, SparseCore 0:
  9.8 29.2 all-gather.2
  150.7 27.9 reduce-scatter.6
  181.0 55.4 all-reduce.5
  250.8 23.7 all-gather.4
  370.4 27.9 reduce-scatter.8
  400.5 55.4 all-reduce.7
where the time goes:
time: 482 us; the launch traced here: 479 us
  waiting for transfers between devices  226 us (47%)
  loops' own time  94.2 us (20%)
  matrix products  66.1 us (14%)
  local copies, waits for them, and re-layouts  47.3 us (10%)
  blocking collectives  20.9 us (4%)
  between operations  17 us (4%)
  other arithmetic  6.63 us (1%)
    psum x2, waiting for transfers between devices, per_device(): sigma = lax.psum(owned, 'term')  115 us
    another operation x2, loops' own time, apply_tasks(): lax.scan(one_task, start, (left_env, right_env, in_sector, out_sector))  94.2 us
    unnamed x8, waiting for transfers between devices  56.8 us
    dynamic_slice x48, local copies, waits for them, and re-layouts, apply_tasks(): lax.scan(one_task, start, (left_env, right_env, in_sector, out_sector))  44 us
    dot_general x24, matrix products, one_task(): jnp.dot(left, block, precision=lax.Precision.HIGHEST, preferred_element_t...  33.9 us
    dot_general x24, matrix products, one_task(): jnp.dot(middle, right, precision=lax.Precision.HIGHEST, preferred_element...  32.1 us
    all_gather x1, waiting for transfers between devices, per_device(): full = lax.all_gather(wavefunction, 'sector', axis=0, tiled=True)  31.1 us
    all_gather x1, waiting for transfers between devices, per_device(): full = lax.all_gather(psi, 'sector', axis=0, tiled=True)  23.8 us
  transfers between devices with their start and end apart: 6, of which 6 were waited for; matrix products, arithmetic and copies ran while one was open for 0% of the time, Pallas kernels for 0%

commit v1 on v0

--- a/solution.py
+++ b/solution.py
@@ -40,7 +40,7 @@
     for step in range(ITERS):
         partial_value = apply_tasks(full, left_env, right_env, in_sector, out_sector)
         owned = lax.psum_scatter(partial_value, "sector", scatter_dimension=0, tiled=True)
-        sigma = lax.psum(owned, "term")
+        sigma = jnp.sum(lax.all_gather(owned, "term"), axis=0)
         updated, res_sq, upd_sq = correction(sigma, psi, precond, shifts[step])
         res_total, upd_total = lax.psum((res_sq, upd_sq), "sector")
         norms.append(jnp.sqrt(res_total))

time: 482 us -> 430 us (0.89)
  waiting for transfers between devices: 226 us -> 173 us
    psum x2 -> x0, waiting for transfers between devices: 115 us -> none  [per_device(): sigma = lax.psum(owned, 'term')]
    all_gather x0 -> x2, waiting for transfers between devices: none -> 60.7 us  [per_device(): sigma = jnp.sum(lax.all_gather(owned, 'term'), axis=0)]
where the time goes in v1:
time: 430 us; the launch traced here: 427 us
  waiting for transfers between devices  173 us (40%)
  loops' own time  94.2 us (22%)
  matrix products  66 us (15%)
  local copies, waits for them, and re-layouts  47.2 us (11%)
  blocking collectives  21 us (5%)
  between operations  17 us (4%)
  other arithmetic  8.42 us (2%)
    another operation x2, loops' own time, apply_tasks(): lax.scan(one_task, start, (left_env, right_env, in_sector, out_sector))  94.2 us
    all_gather x2, waiting for transfers between devices, per_device(): sigma = jnp.sum(lax.all_gather(owned, 'term'), axis=0)  60.7 us
    unnamed x8, waiting for transfers between devices  56.8 us
    dynamic_slice x48, local copies, waits for them, and re-layouts, apply_tasks(): lax.scan(one_task, start, (left_env, right_env, in_sector, out_sector))  43.9 us
    dot_general x24, matrix products, one_task(): jnp.dot(left, block, precision=lax.Precision.HIGHEST, preferred_element_t...  33.9 us
    dot_general x24, matrix products, one_task(): jnp.dot(middle, right, precision=lax.Precision.HIGHEST, preferred_element...  32.1 us
    all_gather x1, waiting for transfers between devices, per_device(): full = lax.all_gather(wavefunction, 'sector', axis=0, tiled=True)  31.1 us
    all_gather x1, waiting for transfers between devices, per_device(): full = lax.all_gather(psi, 'sector', axis=0, tiled=True)  24.2 us
  transfers between devices with their start and end apart: 6, of which 6 were waited for; matrix products, arithmetic and copies ran while one was open for 0% of the time, Pallas kernels for 0%

profile of v1, /device:TPU:0, one launch (start us, length us, event | category | flops | bytes accessed | tf_op | source)
XLA Modules:
  0.0 426.9 jit_solution(15828881781278059368)
XLA Ops:
  7.9 31.1 %all-gather.7.cloned.1.call-done = f32[4,256,256]{2,1,0:T(8,128)} async-done(((f32[1,256,256]{2,1,0:T(8,128)}), f32[4,256,256]{2,1,0:T(8,128)}) %all-gather.7.cloned.1.call-update) | async-done | bytes 1048592 | tf_op jit(solution)/shard_map/all_gather | solution.py:36
  39.2 110.3 %while.20 = (s32[]{:T(128)}, f32[4,256,256]{2,1,0:T(8,128)S(1)}, s32[12]{0:T(128)}, f32[12,256,256]{2,1,0:T(8,128)}, s32[12]{0:T(128)}, /*index=5*/f32[4,256,256...) while((s32[]{:T(128)}, f32[4,256,256]{2,1,0:T(8,128)S(1)}, s32[12]{0:T(128)}, ...), condition=%wide.region_1.2_spmd, body=%wide.region_0.1_spmd.sunk | while | flops 402718720 | bytes 2360525 | solution.py:25
  42.4 1.4 fusion.41
  43.8 1.2 dynamic_slice.81
  47.0 1.3 fusion.42
  51.6 1.4 fusion.41
  56.2 1.3 fusion.42
  60.7 1.4 fusion.41
  62.2 1.2 dynamic_slice.81
  65.4 1.3 fusion.42
  69.9 1.4 fusion.41
  74.6 1.3 fusion.42
  79.1 1.4 fusion.41
  83.8 1.3 fusion.42
  88.3 1.4 fusion.41
  92.9 1.3 fusion.42
  97.5 1.4 fusion.41
  102.1 1.3 fusion.42
  106.7 1.4 fusion.41
  111.3 1.3 fusion.42
  115.9 1.4 fusion.41
  120.5 1.3 fusion.42
  125.1 1.4 fusion.41
  129.7 1.3 fusion.42
  134.2 1.4 fusion.41
  138.9 1.3 fusion.42
  143.4 1.4 fusion.41
  148.1 1.3 fusion.42
  150.5 28.0 %reduce-scatter.7.cloned.1.call-done = f32[1,256,256]{2,1,0:T(8,128)} async-done(((f32[4,256,256]{2,1,0:T(8,128)}), f32[1,256,256]{2,1,0:T(8,128)}) %reduce-scatter.7.cloned.1.call-update) | async-done | bytes 262160
  179.2 30.1 %all-gather.11.cloned.1.call-done = f32[8,256,256]{2,1,0:T(8,128)} async-done(((f32[1,256,256]{2,1,0:T(8,128)}), f32[8,256,256]{2,1,0:T(8,128)}) %all-gather.11.cloned.1.call-update) | async-done | bytes 2097168 | tf_op jit(solution)/shard_map/all_gather | solution.py:43
  209.3 1.8 reduce.2
  211.1 1.5 multiply_reduce_fusion.3
  212.5 10.4 %psum.28 = f32[]{:T(128)} all-reduce(f32[]{:T(128)} %get-tuple-element.111), channel_id=1, replica_groups=mesh['sector'=4,'term'=8] {'sector'}, use_global_device_ids=true, to_apply=%region_5.6 | all-reduce | flops 1 | bytes 8 | tf_op jit(solution)/shard_map/psum | solution.py:45
  224.5 24.2 %all-gather.9.cloned.1.call-done = f32[4,256,256]{2,1,0:T(8,128)} async-done(((f32[1,256,256]{2,1,0:T(8,128)}), f32[4,256,256]{2,1,0:T(8,128)}) %all-gather.9.cloned.1.call-update) | async-done | bytes 1048592 | tf_op jit(solution)/shard_map/all_gather | solution.py:49
  248.8 94.5 %while.21 = (s32[]{:T(128)}, f32[4,256,256]{2,1,0:T(8,128)S(1)}, s32[12]{0:T(128)S(1)}, f32[12,256,256]{2,1,0:T(8,128)}, s32[12]{0:T(128)S(1)}, /*index=5*/f32[4...) while((s32[]{:T(128)}, f32[4,256,256]{2,1,0:T(8,128)S(1)}, ...), condition=%wide.region_7.8_spmd, body=%wide.region_6.7_spmd.sunk | while | flops 402718720 | bytes 2360525 | solution.py:25
  251.3 1.4 fusion.47
  255.3 1.3 fusion.48
  259.2 1.4 fusion.47
  263.2 1.3 fusion.48
  267.1 1.4 fusion.47
  271.0 1.3 fusion.48
  274.9 1.4 fusion.47
  278.9 1.3 fusion.48
  282.8 1.4 fusion.47
  286.8 1.3 fusion.48
  290.7 1.4 fusion.47
  294.7 1.3 fusion.48
  298.6 1.4 fusion.47
  302.6 1.3 fusion.48
  306.4 1.4 fusion.47
  310.4 1.3 fusion.48
  314.3 1.4 fusion.47
  318.3 1.3 fusion.48
  322.2 1.4 fusion.47
  326.2 1.3 fusion.48
  330.1 1.4 fusion.47
  334.1 1.3 fusion.48
  338.0 1.4 fusion.47
  341.9 1.3 fusion.48
  344.4 28.0 %reduce-scatter.9.cloned.1.call-done = f32[1,256,256]{2,1,0:T(8,128)} async-done(((f32[4,256,256]{2,1,0:T(8,128)}), f32[1,256,256]{2,1,0:T(8,128)}) %reduce-scatter.9.cloned.1.call-update) | async-done | bytes 262160
  372.4 30.6 %all-gather.13.cloned.1.call-done = f32[8,256,256]{2,1,0:T(8,128)} async-done(((f32[1,256,256]{2,1,0:T(8,128)}), f32[8,256,256]{2,1,0:T(8,128)}) %all-gather.13.cloned.1.call-update) | async-done | bytes 2097168 | tf_op jit(solution)/shard_map/all_gather | solution.py:43
  403.0 1.8 reduce.3
  404.8 1.4 multiply_reduce_fusion.2
  406.2 10.5 %all-reduce.2 = (f32[]{:T(128)}, f32[]{:T(128)}, f32[]{:T(128)}) all-reduce(f32[]{:T(128)} %get-tuple-element.109, f32[]{:T(128)} %get-tuple-element.114, f32[]{:T(128)} %get-tuple-element.113), channel_id=1, replica_groups=mesh['sector'=4,'term'=8] {'sector'}, use_global_device_ids=true, to_apply=%region_11.12 | all-reduce | flops 3 | bytes 24 | tf_op jit(solution)/shard_map/psum | solution.py:45
  (102 shorter events, 47.7 us)
Async XLA Ops:
  7.2 31.9 %all-gather.7.cloned.1.call-start = ((), (), s32[]{:S(2)}) async-start(), calls=%async_computation.2 | async-start | bytes 1310720 | tf_op jit(solution)/shard_map/all_gather | solution.py:36
  7.9 170.6 %reduce-scatter.7.cloned.1.call-start = ((), (), s32[]{:S(2)}) async-start(), calls=%async_computation.6 | async-start | bytes 1310720
  39.2 139.4 %copy-start.4 = (f32[2]{0:T(128)S(1)}, f32[2]{0:T(128)}, u32[]{:S(2)}) copy-start(f32[2]{0:T(128)} %param.17) | copy-start | bytes 28
  149.4 1.0 copy-start
  149.4 61.6 %copy-start.2 = (f32[1,256,256]{2,1,0:T(8,128)S(1)}, f32[1,256,256]{2,1,0:T(8,128)}, u32[]{:S(2)}) copy-start(f32[1,256,256]{2,1,0:T(8,128)} %param.11) | copy-start | bytes 786436
  149.4 61.6 %copy-start.3 = (f32[1,256,256]{2,1,0:T(8,128)S(1)}, f32[1,256,256]{2,1,0:T(8,128)}, u32[]{:S(2)}) copy-start(f32[1,256,256]{2,1,0:T(8,128)} %param.16) | copy-start | bytes 786436
  149.5 99.3 %copy-start.5 = (s32[12]{0:T(128)S(1)}, s32[12]{0:T(128)}, u32[]{:S(2)}) copy-start(s32[12]{0:T(128)} %get-tuple-element.289) | copy-start | bytes 148
  149.5 99.3 %copy-start.6 = (s32[12]{0:T(128)S(1)}, s32[12]{0:T(128)}, u32[]{:S(2)}) copy-start(s32[12]{0:T(128)} %get-tuple-element.290) | copy-start | bytes 148
  150.4 58.9 %all-gather.11.cloned.1.call-start = ((), (), s32[]{:S(2)}) async-start(), calls=%async_computation.4 | async-start | bytes 2359296 | tf_op jit(solution)/shard_map/all_gather | solution.py:43
  178.5 70.1 %all-gather.9.cloned.1.call-start = ((), (), s32[]{:S(2)}) async-start(), calls=%async_computation.3 | async-start | bytes 1310720 | tf_op jit(solution)/shard_map/all_gather | solution.py:49
  224.4 148.0 %reduce-scatter.9.cloned.1.call-start = ((), (), s32[]{:S(2)}) async-start(), calls=%async_computation.7 | async-start | bytes 1310720
  343.3 1.0 copy-start.1
  344.3 58.7 %all-gather.13.cloned.1.call-start = ((), (), s32[]{:S(2)}) async-start(), calls=%async_computation.5 | async-start | bytes 2359296 | tf_op jit(solution)/shard_map/all_gather | solution.py:43
Sparse Core Ops, SparseCore 0:
  9.8 29.2 all-gather.6
  150.5 27.9 reduce-scatter.6
  180.1 29.1 all-gather.10
  224.5 24.0 all-gather.8
  344.4 27.9 reduce-scatter.8
  373.8 29.1 all-gather.12
